TPU v7x, 32 devices: a whole 2x2x4 slice. The times are simulated.
32 devices in a mesh: blk: 4 (over y, x), uly: 8 (over z, core).
Axes of the slice: x: 2, y: 2, z: 4, core: 2. Of those that a mesh axis runs over, the one named last changes fastest.
Arguments:
- query_proj: bfloat16 [2048, 1024], P(('blk', 'uly')), may hold values from -8 to 8
- key_proj: bfloat16 [2048, 1024], P(('blk', 'uly')), may hold values from -8 to 8
- value_proj: bfloat16 [2048, 1024], P(('blk', 'uly')), may hold values from -6 to 6
- attn_output: bfloat16 [2048, 1024], P(('blk', 'uly')), may hold values from -6 to 6
- out_grad: bfloat16 [2048, 1024], P(('blk', 'uly')), may hold values from -6 to 6
- random_blocks: int32 [16, 3], replicated, may hold values from 0 to 14, as said below
Outputs:
- query_grad: bfloat16 [2048, 1024], P(('blk', 'uly'))
- key_grad: bfloat16 [2048, 1024], P(('blk', 'uly'))
- value_grad: bfloat16 [2048, 1024], P(('blk', 'uly'))
Inputs may be any that keep to these rules, and one draw needn't show every extreme that they name: `random_blocks`: every entry of row i names a block below i; row 0 names only block 0. The rows of one shard of blk (4 rows in a row, aligned) name at most 2 distinct blocks that lie in any one other shard, exactly 2 that lie in the shard just before theirs, and the rows of the last shard name exactly 2 that lie in the first shard.
All inputs are finite; a program needn't handle non-finite values.
Results may differ from a plain program's by a relative error of at most 0.005.
Values may be sent and summed in bfloat16 or wider, within the bound.
A program may use at most 64 MiB of HBM per device.

v0:
```python
import math

import jax
import jax.numpy as jnp
from jax import lax
from jax.sharding import PartitionSpec as P

HD = 128
BLOCK = 128
RAND = 3
CAP = 2


def named_table(random_blocks, per_shard):
    block_count = random_blocks.shape[0]
    shard_count = block_count // per_shard
    entries = random_blocks.reshape(shard_count, per_shard * RAND)
    block_ids = jnp.arange(block_count, dtype=jnp.int32)
    named = jnp.any(entries[:, :, None] == block_ids[None, None, :], axis=1)
    owner = block_ids // per_shard
    named = named & (owner[None, :] != jnp.arange(shard_count, dtype=jnp.int32)[:, None])
    grouped = named.reshape(shard_count, shard_count, per_shard).astype(jnp.int32)
    rank_in = jnp.cumsum(grouped, axis=2) - grouped
    return (grouped, rank_in)


def send_slots(grouped, rank_in, cycle_rank, per_shard):
    mine = lax.dynamic_index_in_dim(grouped, cycle_rank, 1, keepdims=False)
    mine_rank = lax.dynamic_index_in_dim(rank_in, cycle_rank, 1, keepdims=False)
    slot_ids = jnp.arange(CAP, dtype=jnp.int32)
    hit = (mine[:, None, :] == 1) & (mine_rank[:, None, :] == slot_ids[None, :, None])
    positions = jnp.arange(per_shard, dtype=jnp.int32)
    select = jnp.sum(jnp.where(hit, positions[None, None, :], 0), axis=2)
    filled = jnp.any(hit, axis=2)
    return (select, filled)


def on_device(query_proj, key_proj, value_proj, attn_output, out_grad, random_blocks):
    tok_count = query_proj.shape[0]
    head_count = query_proj.shape[1] // HD
    score_scale = HD ** (-0.5)
    extent = 3 + RAND

    def to_heads(tensor):
        return tensor.reshape(tok_count, head_count, HD)

    query_rows, key_rows, value_rows, output_rows, grad_rows = (
        lax.all_to_all(to_heads(query_proj), "uly", split_axis=1, concat_axis=0, tiled=True),
        lax.all_to_all(to_heads(key_proj), "uly", split_axis=1, concat_axis=0, tiled=True),
        lax.all_to_all(to_heads(value_proj), "uly", split_axis=1, concat_axis=0, tiled=True),
        lax.all_to_all(to_heads(attn_output), "uly", split_axis=1, concat_axis=0, tiled=True),
        lax.all_to_all(to_heads(out_grad), "uly", split_axis=1, concat_axis=0, tiled=True),
    )
    row_delta = jnp.sum(
        output_rows.astype(jnp.float32) * grad_rows.astype(jnp.float32), axis=2
    ).reshape(-1)
    shard_len = query_rows.shape[0]
    per_shard = shard_len // BLOCK
    query_blocks = query_rows.reshape(per_shard, BLOCK, HD)
    key_blocks = key_rows.reshape(per_shard, BLOCK, HD)
    value_blocks = value_rows.reshape(per_shard, BLOCK, HD)
    grad_blocks = grad_rows.reshape(per_shard, BLOCK, HD)
    delta_blocks = row_delta.reshape(per_shard, BLOCK)
    cycle_size = lax.axis_size("blk")
    cycle_rank = lax.axis_index("blk")
    block_count = random_blocks.shape[0]
    grouped, rank_in = named_table(random_blocks, per_shard)
    select, filled = send_slots(grouped, rank_in, cycle_rank, per_shard)
    key_send = jnp.where(
        filled[:, :, None, None],
        jnp.take(key_blocks, select.reshape(-1), axis=0).reshape(cycle_size, CAP, BLOCK, HD),
        jnp.zeros((), jnp.bfloat16),
    )
    value_send = jnp.where(
        filled[:, :, None, None],
        jnp.take(value_blocks, select.reshape(-1), axis=0).reshape(cycle_size, CAP, BLOCK, HD),
        jnp.zeros((), jnp.bfloat16),
    )
    extra_key = jnp.broadcast_to(
        jnp.stack([key_blocks[per_shard - 1], key_blocks[0]])[None], (cycle_size, 2, BLOCK, HD)
    )
    extra_value = jnp.broadcast_to(
        jnp.stack([value_blocks[per_shard - 1], value_blocks[0]])[None], (cycle_size, 2, BLOCK, HD)
    )
    all_key, all_value = (
        lax.all_to_all(
            jnp.concatenate([key_send, extra_key], axis=1),
            "blk",
            split_axis=0,
            concat_axis=0,
            tiled=True,
        ),
        lax.all_to_all(
            jnp.concatenate([value_send, extra_value], axis=1),
            "blk",
            split_axis=0,
            concat_axis=0,
            tiled=True,
        ),
    )
    far_key = all_key[:, :CAP]
    far_value = all_value[:, :CAP]
    before_rank = jnp.maximum(cycle_rank - 1, 0)
    prev_key = lax.dynamic_index_in_dim(all_key, before_rank, 0, keepdims=False)[CAP]
    prev_value = lax.dynamic_index_in_dim(all_value, before_rank, 0, keepdims=False)[CAP]
    first_key = all_key[0, CAP + 1]
    first_value = all_value[0, CAP + 1]
    key_store = jnp.concatenate(
        [key_blocks, prev_key[None], first_key[None], far_key.reshape(cycle_size * CAP, BLOCK, HD)],
        axis=0,
    )
    value_store = jnp.concatenate(
        [
            value_blocks,
            prev_value[None],
            first_value[None],
            far_value.reshape(cycle_size * CAP, BLOCK, HD),
        ],
        axis=0,
    )
    store_size = key_store.shape[0]
    picked = lax.dynamic_slice_in_dim(random_blocks, cycle_rank * per_shard, per_shard, 0)
    own_rank = lax.dynamic_index_in_dim(rank_in, cycle_rank, 0, keepdims=False).reshape(-1)
    all_ids = jnp.arange(block_count, dtype=jnp.int32)
    slot_of = jnp.sum(
        jnp.where(picked[:, :, None] == all_ids[None, None, :], own_rank[None, None, :], 0), axis=2
    )
    owner = picked // per_shard
    random_index = jnp.where(
        owner == cycle_rank, picked - cycle_rank * per_shard, per_shard + 2 + owner * CAP + slot_of
    )
    local_ids = jnp.arange(per_shard, dtype=jnp.int32)
    global_ids = cycle_rank * per_shard + local_ids
    listed = jnp.concatenate(
        [
            global_ids[:, None],
            global_ids[:, None] - 1,
            jnp.zeros((per_shard, 1), jnp.int32),
            picked,
        ],
        axis=1,
    )
    first_index = jnp.zeros((per_shard, 1), jnp.int32) + jnp.where(
        cycle_rank == 0, 0, per_shard + 1
    ).astype(jnp.int32)
    store_index = jnp.concatenate(
        [
            local_ids[:, None],
            jnp.where(local_ids >= 1, local_ids - 1, per_shard)[:, None],
            first_index,
            random_index,
        ],
        axis=1,
    )
    order = jnp.arange(extent, dtype=jnp.int32)
    earlier = order[None, :] < order[:, None]
    repeated = jnp.any((listed[:, :, None] == listed[:, None, :]) & earlier[None, :, :], axis=2)
    usable = (listed >= 0) & jnp.logical_not(repeated)
    within = jnp.arange(BLOCK, dtype=jnp.int32)
    group = math.gcd(per_shard, max(1, 512 // BLOCK))
    group_count = per_shard // group

    def group_turn(carry, group_index):
        key_grad_store, value_grad_store = carry
        first = group_index * group
        query_grp = lax.dynamic_slice_in_dim(query_blocks, first, group, 0)
        grad_grp = lax.dynamic_slice_in_dim(grad_blocks, first, group, 0)
        delta_grp = lax.dynamic_slice_in_dim(delta_blocks, first, group, 0)
        index_grp = lax.dynamic_slice_in_dim(store_index, first, group, 0).reshape(-1)
        listed_grp = lax.dynamic_slice_in_dim(listed, first, group, 0)
        usable_grp = lax.dynamic_slice_in_dim(usable, first, group, 0)
        key_sel = jnp.take(key_store, index_grp, axis=0).reshape(group, extent * BLOCK, HD)
        value_sel = jnp.take(value_store, index_grp, axis=0).reshape(group, extent * BLOCK, HD)
        scores = (
            jnp.einsum("gqd,gkd->gqk", query_grp, key_sel, preferred_element_type=jnp.float32)
            * score_scale
        )
        query_pos = (cycle_rank * per_shard + first + jnp.arange(group, dtype=jnp.int32))[
            :, None
        ] * BLOCK + within[None, :]
        key_pos = (listed_grp[:, :, None] * BLOCK + within[None, None, :]).reshape(
            group, extent * BLOCK
        )
        allowed = jnp.repeat(usable_grp, BLOCK, axis=1)[:, None, :] & (
            key_pos[:, None, :] <= query_pos[:, :, None]
        )
        row_max = jnp.max(jnp.where(allowed, scores, -1e30), axis=2)
        total = jnp.sum(jnp.where(allowed, jnp.exp(scores - row_max[:, :, None]), 0.0), axis=2)
        log_total = row_max + jnp.log(total)
        probs = jnp.where(allowed, jnp.exp(scores - log_total[:, :, None]), 0.0)
        prob_grad = jnp.einsum(
            "gqd,gkd->gqk", grad_grp, value_sel, preferred_element_type=jnp.float32
        )
        score_grad = (probs * (prob_grad - delta_grp[:, :, None]) * score_scale).astype(
            jnp.bfloat16
        )
        query_part = jnp.einsum(
            "gqk,gkd->gqd", score_grad, key_sel, preferred_element_type=jnp.float32
        ).astype(jnp.bfloat16)
        key_part = jnp.einsum(
            "gqk,gqd->gkd", score_grad, query_grp, preferred_element_type=jnp.float32
        )
        value_part = jnp.einsum(
            "gqk,gqd->gkd", probs.astype(jnp.bfloat16), grad_grp, preferred_element_type=jnp.float32
        )
        key_grad_store = key_grad_store.at[index_grp].add(
            key_part.reshape(group * extent, BLOCK, HD)
        )
        value_grad_store = value_grad_store.at[index_grp].add(
            value_part.reshape(group * extent, BLOCK, HD)
        )
        return ((key_grad_store, value_grad_store), query_part)

    zero_store = jnp.zeros((store_size, BLOCK, HD), jnp.float32)
    (key_grad_store, value_grad_store), query_parts = lax.scan(
        group_turn, (zero_store, zero_store), jnp.arange(group_count, dtype=jnp.int32)
    )
    query_acc = query_parts.reshape(shard_len, HD)
    key_acc = key_grad_store[:per_shard]
    value_acc = value_grad_store[:per_shard]
    far_key_grad = key_grad_store[per_shard + 2 :].reshape(cycle_size, CAP, BLOCK, HD)
    far_value_grad = value_grad_store[per_shard + 2 :].reshape(cycle_size, CAP, BLOCK, HD)
    dest_ids = jnp.arange(cycle_size, dtype=jnp.int32)
    to_prev = (dest_ids == cycle_rank - 1)[:, None, None]
    to_first = (dest_ids == 0)[:, None, None]
    extra_key_grad = jnp.stack(
        [
            jnp.where(to_prev, key_grad_store[per_shard][None], 0.0),
            jnp.where(to_first, key_grad_store[per_shard + 1][None], 0.0),
        ],
        axis=1,
    )
    extra_value_grad = jnp.stack(
        [
            jnp.where(to_prev, value_grad_store[per_shard][None], 0.0),
            jnp.where(to_first, value_grad_store[per_shard + 1][None], 0.0),
        ],
        axis=1,
    )
    all_key_back, all_value_back = (
        lax.all_to_all(
            jnp.concatenate([far_key_grad, extra_key_grad], axis=1),
            "blk",
            split_axis=0,
            concat_axis=0,
            tiled=True,
        ),
        lax.all_to_all(
            jnp.concatenate([far_value_grad, extra_value_grad], axis=1),
            "blk",
            split_axis=0,
            concat_axis=0,
            tiled=True,
        ),
    )
    back_key = all_key_back[:, :CAP]
    back_value = all_value_back[:, :CAP]
    prev_back = jnp.stack(
        [jnp.sum(all_key_back[:, CAP], axis=0), jnp.sum(all_value_back[:, CAP], axis=0)]
    )
    first_back = jnp.stack(
        [jnp.sum(all_key_back[:, CAP + 1], axis=0), jnp.sum(all_value_back[:, CAP + 1], axis=0)]
    )
    key_acc = key_acc.at[per_shard - 1].add(prev_back[0]).at[0].add(first_back[0])
    value_acc = value_acc.at[per_shard - 1].add(prev_back[1]).at[0].add(first_back[1])
    back_key = jnp.where(filled[:, :, None, None], back_key, 0.0).reshape(
        cycle_size * CAP, BLOCK, HD
    )
    back_value = jnp.where(filled[:, :, None, None], back_value, 0.0).reshape(
        cycle_size * CAP, BLOCK, HD
    )
    key_acc = key_acc.at[select.reshape(-1)].add(back_key).reshape(shard_len, HD)
    value_acc = value_acc.at[select.reshape(-1)].add(back_value).reshape(shard_len, HD)
    outgoing = (
        query_acc.reshape(shard_len, 1, HD),
        key_acc.astype(jnp.bfloat16).reshape(shard_len, 1, HD),
        value_acc.astype(jnp.bfloat16).reshape(shard_len, 1, HD),
    )
    query_back, key_back, value_back = (
        lax.all_to_all(outgoing[0], "uly", split_axis=0, concat_axis=1, tiled=True),
        lax.all_to_all(outgoing[1], "uly", split_axis=0, concat_axis=1, tiled=True),
        lax.all_to_all(outgoing[2], "uly", split_axis=0, concat_axis=1, tiled=True),
    )
    return (
        query_back.reshape(tok_count, head_count * HD),
        key_back.reshape(tok_count, head_count * HD),
        value_back.reshape(tok_count, head_count * HD),
    )


def solution(mesh):
    return jax.shard_map(
        on_device,
        mesh=mesh,
        in_specs=(
            P(("blk", "uly"), None),
            P(("blk", "uly"), None),
            P(("blk", "uly"), None),
            P(("blk", "uly"), None),
            P(("blk", "uly"), None),
            P(),
        ),
        out_specs=(P(("blk", "uly"), None), P(("blk", "uly"), None), P(("blk", "uly"), None)),
        check_vma=False,
    )
```

profile of v0, /device:TPU:0, one launch (start us, length us, event | category | flops | bytes accessed | tf_op | source)
XLA Modules:
  0.0 171.1 jit_solution(17806742375799658271)
XLA Ops:
  2.2 6.4 %all-to-all-start = ((bf16[64,8,128]{2,0,1:T(8,128)(2,1)}), bf16[64,8,128]{2,0,1:T(8,128)(2,1)S(1)}, u32[]{:S(2)}, u32[]{:S(2)}) async-start(bf16[64,8,128]{2,0,1:T(8,128)(2,1)} %copy_bitcast_fusion.7), calls=%async_computation | async-start | bytes 262144 | tf_op jit(solution)/shard_map/all_to_all | solution.py:49
  18.7 5.1 %all-to-all-start.3 = ((bf16[64,8,128]{2,0,1:T(8,128)(2,1)}), bf16[64,8,128]{2,0,1:T(8,128)(2,1)S(1)}, u32[]{:S(2)}, u32[]{:S(2)}) async-start(bf16[64,8,128]{2,0,1:T(8,128)(2,1)} %copy_bitcast_fusion.5), calls=%async_computation.3 | async-start | bytes 262144 | tf_op jit(solution)/shard_map/all_to_all | solution.py:50
  25.1 5.5 %all-to-all-done.3 = bf16[64,8,128]{2,0,1:T(8,128)(2,1)S(1)} async-done(((bf16[64,8,128]{2,0,1:T(8,128)(2,1)}), bf16[64,8,128]{2,0,1:T(8,128)(2,1)S(1)}, u32[]{:S(2)}, u32[]{:S(2)}) %all-to-all-start.3) | async-done | bytes 131104 | tf_op jit(solution)/shard_map/all_to_all | solution.py:50
  30.6 3.4 %all-to-all-start.5 = ((bf16[64,8,128]{2,0,1:T(8,128)(2,1)}), bf16[64,8,128]{2,0,1:T(8,128)(2,1)S(1)}, u32[]{:S(2)}, u32[]{:S(2)}) async-start(bf16[64,8,128]{2,0,1:T(8,128)(2,1)} %copy_bitcast_fusion.4), calls=%async_computation.5 | async-start | bytes 262144 | tf_op jit(solution)/shard_map/all_to_all | solution.py:52
  34.8 5.8 %all-to-all-done.5 = bf16[64,8,128]{2,0,1:T(8,128)(2,1)S(1)} async-done(((bf16[64,8,128]{2,0,1:T(8,128)(2,1)}), bf16[64,8,128]{2,0,1:T(8,128)(2,1)S(1)}, u32[]{:S(2)}, u32[]{:S(2)}) %all-to-all-start.5) | async-done | bytes 131104 | tf_op jit(solution)/shard_map/all_to_all | solution.py:52
  40.7 3.4 %all-to-all-start.6 = ((bf16[64,8,128]{2,0,1:T(8,128)(2,1)}), bf16[64,8,128]{2,0,1:T(8,128)(2,1)S(1)}, u32[]{:S(2)}, u32[]{:S(2)}) async-start(bf16[64,8,128]{2,0,1:T(8,128)(2,1)} %copy_bitcast_fusion.3), calls=%async_computation.6 | async-start | bytes 262144 | tf_op jit(solution)/shard_map/all_to_all | solution.py:51
  44.9 5.8 %all-to-all-done.6 = bf16[64,8,128]{2,0,1:T(8,128)(2,1)S(1)} async-done(((bf16[64,8,128]{2,0,1:T(8,128)(2,1)}), bf16[64,8,128]{2,0,1:T(8,128)(2,1)S(1)}, u32[]{:S(2)}, u32[]{:S(2)}) %all-to-all-start.6) | async-done | bytes 131104 | tf_op jit(solution)/shard_map/all_to_all | solution.py:51
  50.7 3.7 %all-to-all-start.1 = ((bf16[4,4,128,128]{3,2,1,0:T(8,128)(2,1)}), bf16[4,4,128,128]{3,2,1,0:T(8,128)(2,1)S(1)}, u32[]{:S(2)}, u32[]{:S(2)}) async-start(bf16[4,4,128,128]{3,2,1,0:T(8,128)(2,1)} %pad_maximum_fusion.2), calls=%async_computation.1 | async-start | bytes 1048576 | tf_op jit(solution)/shard_map/all_to_all | solution.py:86
  55.3 6.8 %all-to-all-done.1 = bf16[4,4,128,128]{3,2,1,0:T(8,128)(2,1)S(1)} async-done(((bf16[4,4,128,128]{3,2,1,0:T(8,128)(2,1)}), bf16[4,4,128,128]{3,2,1,0:T(8,128)(2,1)S(1)}, u32[]{:S(2)}, u32[]{:S(2)}) %all-to-all-start.1) | async-done | bytes 524320 | tf_op jit(solution)/shard_map/all_to_all | solution.py:86
  62.2 3.5 %all-to-all-start.4 = ((bf16[4,4,128,128]{3,2,1,0:T(8,128)(2,1)}), bf16[4,4,128,128]{3,2,1,0:T(8,128)(2,1)S(1)}, u32[]{:S(2)}, u32[]{:S(2)}) async-start(bf16[4,4,128,128]{3,2,1,0:T(8,128)(2,1)} %pad_maximum_fusion.3), calls=%async_computation.4 | async-start | bytes 1048576 | tf_op jit(solution)/shard_map/all_to_all | solution.py:93
  67.7 4.9 %all-to-all-done.4 = bf16[4,4,128,128]{3,2,1,0:T(8,128)(2,1)S(1)} async-done(((bf16[4,4,128,128]{3,2,1,0:T(8,128)(2,1)}), bf16[4,4,128,128]{3,2,1,0:T(8,128)(2,1)S(1)}, u32[]{:S(2)}, u32[]{:S(2)}) %all-to-all-start.4) | async-done | bytes 524320 | tf_op jit(solution)/shard_map/all_to_all | solution.py:93
  72.6 3.4 %all-to-all-start.2 = ((bf16[64,8,128]{2,0,1:T(8,128)(2,1)}), bf16[64,8,128]{2,0,1:T(8,128)(2,1)S(1)}, u32[]{:S(2)}, u32[]{:S(2)}) async-start(bf16[64,8,128]{2,0,1:T(8,128)(2,1)} %copy_bitcast_fusion.6), calls=%async_computation.2 | async-start | bytes 262144 | tf_op jit(solution)/shard_map/all_to_all | solution.py:48
  78.7 4.0 %all-to-all-done.2 = bf16[64,8,128]{2,0,1:T(8,128)(2,1)S(1)} async-done(((bf16[64,8,128]{2,0,1:T(8,128)(2,1)}), bf16[64,8,128]{2,0,1:T(8,128)(2,1)S(1)}, u32[]{:S(2)}, u32[]{:S(2)}) %all-to-all-start.2) | async-done | bytes 131104 | tf_op jit(solution)/shard_map/all_to_all | solution.py:48
  85.2 2.3 %fusion.9 = f32[4,768,128]{2,1,0:T(8,128)S(1)} fusion(bf16[4,128,128]{2,1,0:T(8,128)(2,1)S(1)} %bitcast.196, f32[4,768,128]{2,1,0:T(8,128)S(1)} %get-tuple-element.126, f32[4,128]{1,0:T(4,128)S(1)} %log_add_fusion, s32[4,128]{1,0:T(4,128)} %copy-done.15, s32[4,768]{1,0:T(4,128)S(1)} %bitcast_add_fusion, pred[4,768]{1,0:T(4,128)(4,1)S(1)} %bitcast.223), kind=kOutput, calls=%fused_computation.26 | convolution fusion | flops 102629376 | bytes 3296256 | tf_op jit(solution)/shard_map/while/body/eval_jaxpr/gqk,gqd->gkd/dot_general | solution.py:203
  90.5 4.5 %scatter_fusion = f32[14,128,128]{2,1,0:T(8,128)S(1)} fusion(f32[14,128,128]{2,1,0:T(8,128)S(1)} %broadcast_in_dim.228.clone, s32[24]{0:T(128)S(1)} %copy-done.19, f32[24,128,128]{2,1,0:T(8,128)} %bitcast.183), kind=kCustom, calls=%fused_computation.4 | custom fusion | flops 393216 | bytes 4718688 | tf_op jit(solution)/shard_map/while/body/eval_jaxpr/scatter-add | solution.py:206
  96.6 2.6 %scatter_fusion.2 = f32[14,128,128]{2,1,0:T(8,128)S(1)} fusion(f32[14,128,128]{2,1,0:T(8,128)S(1)} %broadcast_in_dim.228.clone.1, s32[24]{0:T(128)S(1)} %copy-done.19, f32[24,128,128]{2,1,0:T(8,128)S(1)} %bitcast.182), kind=kCustom, calls=%fused_computation.6 | custom fusion | flops 393216 | bytes 4718688 | tf_op jit(solution)/shard_map/while/body/eval_jaxpr/scatter-add | solution.py:209
  99.2 1.7 broadcast_select_fusion.6
  100.9 1.7 broadcast_select_fusion.7
  103.7 3.6 %all-to-all-start.8 = ((f32[4,4,128,128]{3,2,1,0:T(8,128)}), f32[4,4,128,128]{3,2,1,0:T(8,128)S(1)}, u32[]{:S(2)}, u32[]{:S(2)}) async-start(f32[4,4,128,128]{3,2,1,0:T(8,128)} %pad_maximum_fusion), calls=%async_computation.8 | async-start | bytes 2097152 | tf_op jit(solution)/shard_map/all_to_all | solution.py:241
  109.6 11.4 %all-to-all-done.8 = f32[4,4,128,128]{3,2,1,0:T(8,128)S(1)} async-done(((f32[4,4,128,128]{3,2,1,0:T(8,128)}), f32[4,4,128,128]{3,2,1,0:T(8,128)S(1)}, u32[]{:S(2)}, u32[]{:S(2)}) %all-to-all-start.8) | async-done | bytes 1048608 | tf_op jit(solution)/shard_map/all_to_all | solution.py:241
  120.9 4.2 %all-to-all-start.10 = ((f32[4,4,128,128]{3,2,1,0:T(8,128)}), f32[4,4,128,128]{3,2,1,0:T(8,128)}, u32[]{:S(2)}, u32[]{:S(2)}) async-start(f32[4,4,128,128]{3,2,1,0:T(8,128)} %pad_maximum_fusion.1), calls=%async_computation.10 | async-start | bytes 2097152 | tf_op jit(solution)/shard_map/all_to_all | solution.py:248
  125.2 2.4 %convolution_convert_fusion = bf16[4,128,128]{2,1,0:T(8,128)(2,1)} fusion(bf16[4,128,768]{1,2,0:T(8,128)(2,1)} %copy-done.1, bf16[4,768,128]{2,1,0:T(8,128)(2,1)} %bitcast.185), kind=kOutput, calls=%fused_computation.22 | convolution fusion | flops 100728832 | bytes 1703936 | tf_op jit(solution)/shard_map/while/body/eval_jaxpr/gqk,gkd->gqd/dot_general | solution.py:197
  128.1 2.3 %reduce.14 = bf16[512,128]{1,0:T(8,128)(2,1)} reduce(bf16[512,1,128]{2,0,1:T(8,128)(2,1)} %bitcast.213, bf16[]{:T(256)} %broadcast.500), dimensions={1}, to_apply=%copy.127.reduce_sub_computation | reduce | bytes 262146 | tf_op jit(solution)/shard_map/reshape;reshape | solution.py:275
  130.4 1.6 reshape.619
  132.1 6.3 %all-to-all-done.10 = f32[4,4,128,128]{3,2,1,0:T(8,128)} async-done(((f32[4,4,128,128]{3,2,1,0:T(8,128)}), f32[4,4,128,128]{3,2,1,0:T(8,128)}, u32[]{:S(2)}, u32[]{:S(2)}) %all-to-all-start.10) | async-done | bytes 1048608 | tf_op jit(solution)/shard_map/all_to_all | solution.py:248
  138.4 3.4 %all-to-all-start.7 = ((bf16[8,2,4096]{2,1,0:T(2,128)(2,1)}), bf16[8,2,4096]{2,1,0:T(2,128)(2,1)S(1)}, u32[]{:S(2)}, u32[]{:S(2)}) async-start(bf16[8,2,4096]{2,1,0:T(2,128)(2,1)} %reshape.619), calls=%async_computation.7 | async-start | bytes 262144 | tf_op jit(solution)/shard_map/all_to_all | solution.py:280
  141.8 2.0 %slice_select_fusion = (f32[4,2,128,128]{3,2,1,0:T(8,128)S(1)}, f32[4,2,128,128]{3,2,1,0:T(8,128)}) fusion(f32[4,4,128,128]{3,2,1,0:T(8,128)} %all-to-all-done.10, pred[4,2]{1,0:T(4,128)(4,1)S(1)} %copy-done.18, f32[4,4,128,128]{3,2,1,0:T(8,128)S(1)} %all-to-all-done.8), kind=kLoop, calls=%fused_computation.34 | loop fusion | flops 262144 | bytes 2097160 | tf_op jit(solution)/shard_map/jit(_where)/select_n | solution.py:269
  144.9 2.0 %scatter_fusion.1 = f32[4,128,128]{2,1,0:T(8,128)S(1)} fusion(f32[4,128,128]{2,1,0:T(8,128)S(1)} %fusion.20, s32[8]{0:T(128)S(1)} %fusion.32, f32[8,128,128]{2,1,0:T(8,128)} %bitcast.193), kind=kCustom, calls=%fused_computation.5 | custom fusion | flops 131072 | bytes 1572896 | tf_op jit(solution)/shard_map/scatter-add | solution.py:272
  148.4 4.9 %all-to-all-start.9 = ((bf16[8,2,4096]{2,1,0:T(2,128)(2,1)}), bf16[8,2,4096]{2,1,0:T(2,128)(2,1)S(1)}, u32[]{:S(2)}, u32[]{:S(2)}) async-start(bf16[8,2,4096]{2,1,0:T(2,128)(2,1)} %reshape.621), calls=%async_computation.9 | async-start | bytes 262144 | tf_op jit(solution)/shard_map/all_to_all | solution.py:281
  155.8 4.3 %all-to-all-done.9 = bf16[8,2,4096]{2,1,0:T(2,128)(2,1)S(1)} async-done(((bf16[8,2,4096]{2,1,0:T(2,128)(2,1)}), bf16[8,2,4096]{2,1,0:T(2,128)(2,1)S(1)}, u32[]{:S(2)}, u32[]{:S(2)}) %all-to-all-start.9) | async-done | bytes 131104 | tf_op jit(solution)/shard_map/all_to_all | solution.py:281
  160.1 3.4 %all-to-all-start.11 = ((bf16[8,2,4096]{2,1,0:T(2,128)(2,1)}), bf16[8,2,4096]{2,1,0:T(2,128)(2,1)S(1)}, u32[]{:S(2)}, u32[]{:S(2)}) async-start(bf16[8,2,4096]{2,1,0:T(2,128)(2,1)} %reshape.623), calls=%async_computation.11 | async-start | bytes 262144 | tf_op jit(solution)/shard_map/all_to_all | solution.py:282
  165.3 4.8 %all-to-all-done.11 = bf16[8,2,4096]{2,1,0:T(2,128)(2,1)S(1)} async-done(((bf16[8,2,4096]{2,1,0:T(2,128)(2,1)}), bf16[8,2,4096]{2,1,0:T(2,128)(2,1)S(1)}, u32[]{:S(2)}, u32[]{:S(2)}) %all-to-all-start.11) | async-done | bytes 131104 | tf_op jit(solution)/shard_map/all_to_all | solution.py:282
  (172 shorter events, 38.7 us)
Async XLA Ops:
  0.6 23.2 %copy-start.11 = (bf16[64,1024]{1,0:T(8,128)(2,1)S(1)}, bf16[64,1024]{1,0:T(8,128)(2,1)}, u32[]{:S(2)}) copy-start(bf16[64,1024]{1,0:T(8,128)(2,1)} %param.21) | copy-start | bytes 393220
  2.2 16.5 %all-to-all-start = ((bf16[64,8,128]{2,0,1:T(8,128)(2,1)}), bf16[64,8,128]{2,0,1:T(8,128)(2,1)S(1)}, u32[]{:S(2)}, u32[]{:S(2)}) async-start(bf16[64,8,128]{2,0,1:T(8,128)(2,1)} %copy_bitcast_fusion.7), calls=%async_computation | async-start | bytes 262144 | tf_op jit(solution)/shard_map/all_to_all | solution.py:49
  10.7 2.2 %copy-start.13 = (s32[4,2]{1,0:T(4,128)}, s32[4,2]{1,0:T(4,128)S(1)}, u32[]{:S(2)}) copy-start(s32[4,2]{1,0:T(4,128)S(1)} %copy.121) | copy-start | bytes 100
  15.6 19.1 %copy-start.17 = (pred[4,2]{1,0:T(4,128)(4,1)}, pred[4,2]{1,0:T(4,128)(4,1)S(1)}, u32[]{:S(2)}) copy-start(pred[4,2]{1,0:T(4,128)(4,1)S(1)} %copy.120) | copy-start | bytes 28
  15.6 68.3 %copy-start.15 = (s32[4,128]{1,0:T(4,128)}, s32[4,128]{1,0:T(4,128)S(1)}, u32[]{:S(2)}) copy-start(s32[4,128]{1,0:T(4,128)S(1)} %iota_add_fusion) | copy-start | bytes 6148
  18.7 11.8 %all-to-all-start.3 = ((bf16[64,8,128]{2,0,1:T(8,128)(2,1)}), bf16[64,8,128]{2,0,1:T(8,128)(2,1)S(1)}, u32[]{:S(2)}, u32[]{:S(2)}) async-start(bf16[64,8,128]{2,0,1:T(8,128)(2,1)} %copy_bitcast_fusion.5), calls=%async_computation.3 | async-start | bytes 262144 | tf_op jit(solution)/shard_map/all_to_all | solution.py:50
  30.6 10.1 %all-to-all-start.5 = ((bf16[64,8,128]{2,0,1:T(8,128)(2,1)}), bf16[64,8,128]{2,0,1:T(8,128)(2,1)S(1)}, u32[]{:S(2)}, u32[]{:S(2)}) async-start(bf16[64,8,128]{2,0,1:T(8,128)(2,1)} %copy_bitcast_fusion.4), calls=%async_computation.5 | async-start | bytes 262144 | tf_op jit(solution)/shard_map/all_to_all | solution.py:52
  40.7 26.2 %copy-start.4 = (bf16[64,8,128]{2,0,1:T(8,128)(2,1)}, bf16[64,8,128]{2,0,1:T(8,128)(2,1)S(1)}, u32[]{:S(2)}) copy-start(bf16[64,8,128]{2,0,1:T(8,128)(2,1)S(1)} %all-to-all-done.5) | copy-start | bytes 393220
  40.7 10.1 %all-to-all-start.6 = ((bf16[64,8,128]{2,0,1:T(8,128)(2,1)}), bf16[64,8,128]{2,0,1:T(8,128)(2,1)S(1)}, u32[]{:S(2)}, u32[]{:S(2)}) async-start(bf16[64,8,128]{2,0,1:T(8,128)(2,1)} %copy_bitcast_fusion.3), calls=%async_computation.6 | async-start | bytes 262144 | tf_op jit(solution)/shard_map/all_to_all | solution.py:51
  50.7 11.4 %all-to-all-start.1 = ((bf16[4,4,128,128]{3,2,1,0:T(8,128)(2,1)}), bf16[4,4,128,128]{3,2,1,0:T(8,128)(2,1)S(1)}, u32[]{:S(2)}, u32[]{:S(2)}) async-start(bf16[4,4,128,128]{3,2,1,0:T(8,128)(2,1)} %pad_maximum_fusion.2), calls=%async_computation.1 | async-start | bytes 1048576 | tf_op jit(solution)/shard_map/all_to_all | solution.py:86
  54.4 11.8 %copy-start.12 = (bf16[64,1024]{1,0:T(8,128)(2,1)S(1)}, bf16[64,1024]{1,0:T(8,128)(2,1)}, u32[]{:S(2)}) copy-start(bf16[64,1024]{1,0:T(8,128)(2,1)} %param.18) | copy-start | bytes 393220
  62.2 10.4 %all-to-all-start.4 = ((bf16[4,4,128,128]{3,2,1,0:T(8,128)(2,1)}), bf16[4,4,128,128]{3,2,1,0:T(8,128)(2,1)S(1)}, u32[]{:S(2)}, u32[]{:S(2)}) async-start(bf16[4,4,128,128]{3,2,1,0:T(8,128)(2,1)} %pad_maximum_fusion.3), calls=%async_computation.4 | async-start | bytes 1048576 | tf_op jit(solution)/shard_map/all_to_all | solution.py:93
  72.6 10.1 %all-to-all-start.2 = ((bf16[64,8,128]{2,0,1:T(8,128)(2,1)}), bf16[64,8,128]{2,0,1:T(8,128)(2,1)S(1)}, u32[]{:S(2)}, u32[]{:S(2)}) async-start(bf16[64,8,128]{2,0,1:T(8,128)(2,1)} %copy_bitcast_fusion.6), calls=%async_computation.2 | async-start | bytes 262144 | tf_op jit(solution)/shard_map/all_to_all | solution.py:48
  78.6 5.3 %copy-start.2 = (bf16[24,128,128]{2,1,0:T(8,128)(2,1)}, bf16[24,128,128]{2,1,0:T(8,128)(2,1)S(1)}, u32[]{:S(2)}) copy-start(bf16[24,128,128]{2,1,0:T(8,128)(2,1)S(1)} %get-tuple-element.119) | copy-start | bytes 2359300
  82.7 1.3 copy-start.9
  84.0 1.2 copy-start.5
  85.2 2.4 %copy-start.8 = (bf16[24,128,128]{2,1,0:T(8,128)(2,1)S(1)}, bf16[24,128,128]{2,1,0:T(8,128)(2,1)}, u32[]{:S(2)}) copy-start(bf16[24,128,128]{2,1,0:T(8,128)(2,1)} %get-tuple-element.120) | copy-start | bytes 2359300
  85.2 2.4 %copy-start.16 = (s32[4,128]{1,0:T(4,128)S(1)}, s32[4,128]{1,0:T(4,128)}, u32[]{:S(2)}) copy-start(s32[4,128]{1,0:T(4,128)} %copy-done.15) | copy-start | bytes 6148
  85.2 2.4 %copy-start.20 = (f32[4,128]{1,0:T(4,128)S(1)}, f32[4,128]{1,0:T(4,128)}, u32[]{:S(2)}) copy-start(f32[4,128]{1,0:T(4,128)} %sub.80) | copy-start | bytes 6148
  87.6 1.3 copy-start.10
  88.9 1.5 copy-start.1
  88.9 1.6 copy-start.19
  96.6 2.7 %copy-start.21 = (pred[4]{0:T(512)(128)(4,1)S(1)}, pred[4]{0:T(512)(128)(4,1)}, u32[]{:S(2)}) copy-start(pred[4]{0:T(512)(128)(4,1)} %iota_compare_fusion.5) | copy-start | bytes 16
  96.6 4.4 %copy-start.22 = (pred[4]{0:T(512)(128)(4,1)S(1)}, pred[4]{0:T(512)(128)(4,1)}, u32[]{:S(2)}) copy-start(pred[4]{0:T(512)(128)(4,1)} %iota_compare_fusion.6) | copy-start | bytes 16
  99.2 3.4 %copy-start.3 = (f32[8,128,128]{2,1,0:T(8,128)S(1)}, f32[8,128,128]{2,1,0:T(8,128)}, u32[]{:S(2)}) copy-start(f32[8,128,128]{2,1,0:T(8,128)} %slice.232) | copy-start | bytes 1572868
  103.7 3.7 %copy-start.14 = (s32[4,2]{1,0:T(4,128)S(1)}, s32[4,2]{1,0:T(4,128)}, u32[]{:S(2)}) copy-start(s32[4,2]{1,0:T(4,128)} %copy-done.13) | copy-start | bytes 100
  103.7 17.2 %all-to-all-start.8 = ((f32[4,4,128,128]{3,2,1,0:T(8,128)}), f32[4,4,128,128]{3,2,1,0:T(8,128)S(1)}, u32[]{:S(2)}, u32[]{:S(2)}) async-start(f32[4,4,128,128]{3,2,1,0:T(8,128)} %pad_maximum_fusion), calls=%async_computation.8 | async-start | bytes 2097152 | tf_op jit(solution)/shard_map/all_to_all | solution.py:241
  120.9 17.4 %all-to-all-start.10 = ((f32[4,4,128,128]{3,2,1,0:T(8,128)}), f32[4,4,128,128]{3,2,1,0:T(8,128)}, u32[]{:S(2)}, u32[]{:S(2)}) async-start(f32[4,4,128,128]{3,2,1,0:T(8,128)} %pad_maximum_fusion.1), calls=%async_computation.10 | async-start | bytes 2097152 | tf_op jit(solution)/shard_map/all_to_all | solution.py:248
  125.2 16.6 %copy-start.18 = (pred[4,2]{1,0:T(4,128)(4,1)S(1)}, pred[4,2]{1,0:T(4,128)(4,1)}, u32[]{:S(2)}) copy-start(pred[4,2]{1,0:T(4,128)(4,1)} %copy-done.17) | copy-start | bytes 28
  138.4 10.1 %all-to-all-start.7 = ((bf16[8,2,4096]{2,1,0:T(2,128)(2,1)}), bf16[8,2,4096]{2,1,0:T(2,128)(2,1)S(1)}, u32[]{:S(2)}, u32[]{:S(2)}) async-start(bf16[8,2,4096]{2,1,0:T(2,128)(2,1)} %reshape.619), calls=%async_computation.7 | async-start | bytes 262144 | tf_op jit(solution)/shard_map/all_to_all | solution.py:280
  148.4 11.6 %all-to-all-start.9 = ((bf16[8,2,4096]{2,1,0:T(2,128)(2,1)}), bf16[8,2,4096]{2,1,0:T(2,128)(2,1)S(1)}, u32[]{:S(2)}, u32[]{:S(2)}) async-start(bf16[8,2,4096]{2,1,0:T(2,128)(2,1)} %reshape.621), calls=%async_computation.9 | async-start | bytes 262144 | tf_op jit(solution)/shard_map/all_to_all | solution.py:281
  160.1 10.1 %all-to-all-start.11 = ((bf16[8,2,4096]{2,1,0:T(2,128)(2,1)}), bf16[8,2,4096]{2,1,0:T(2,128)(2,1)S(1)}, u32[]{:S(2)}, u32[]{:S(2)}) async-start(bf16[8,2,4096]{2,1,0:T(2,128)(2,1)} %reshape.623), calls=%async_computation.11 | async-start | bytes 262144 | tf_op jit(solution)/shard_map/all_to_all | solution.py:282
  (3 other events, 2.9 us)
where the time goes:
time: 173 us; the launch traced here: 171 us
  waiting for transfers between devices  59.7 us (35%)
  starting transfers between devices  48.3 us (28%)
  other arithmetic  31.3 us (18%)
  local copies, waits for them, and re-layouts  21.6 us (12%)
  matrix products  8.85 us (5%)
    all_to_all x1, waiting for transfers between devices, on_device(): lax.all_to_all(jnp.concatenate([far_key_grad, extra_key_grad], axis=1), '...  11.4 us
    unnamed x63, local copies, waits for them, and re-layouts  8.27 us
    all_to_all x1, waiting for transfers between devices, on_device(): lax.all_to_all(jnp.concatenate([key_send, extra_key], axis=1), 'blk', spl...  6.83 us
    all_to_all x1, starting transfers between devices, on_device(): lax.all_to_all(to_heads(key_proj), 'uly', split_axis=1, concat_axis=0, ti...  6.35 us
    all_to_all x1, waiting for transfers between devices, on_device(): lax.all_to_all(jnp.concatenate([far_value_grad, extra_value_grad], axis=1...  6.32 us
    all_to_all x1, waiting for transfers between devices, on_device(): lax.all_to_all(to_heads(out_grad), 'uly', split_axis=1, concat_axis=0, ti...  5.82 us
    all_to_all x1, waiting for transfers between devices, on_device(): lax.all_to_all(to_heads(attn_output), 'uly', split_axis=1, concat_axis=0,...  5.79 us
    all_to_all x1, waiting for transfers between devices, on_device(): lax.all_to_all(to_heads(value_proj), 'uly', split_axis=1, concat_axis=0,...  5.47 us
  transfers between devices with their start and end apart: 12, of which 11 were waited for; matrix products, arithmetic and copies ran while one was open for 22% of the time, Pallas kernels for 0%

commit v1 on v0

--- a/solution.py
+++ b/solution.py
@@ -1,8 +1,11 @@
+import functools
 import math
 
 import jax
 import jax.numpy as jnp
 from jax import lax
+from jax.experimental import pallas as pl
+from jax.experimental.pallas import tpu as pltpu
 from jax.sharding import PartitionSpec as P
 
 HD = 128
@@ -288,9 +291,414 @@
     )
 
 
+NEG = -1e30
+KEY, QUERY, VALUE, GRAD = 0, 1, 2, 3
+ROWS_BY_COLS = (((1,), (1,)), ((), ()))
+COLS_BY_COLS = (((0,), (0,)), ((), ()))
+
+
+def swing(count):
+    offsets = [0]
+    for step in range(1, count):
+        offsets.append((step + 1) // 2 if step % 2 else count - step // 2)
+    return offsets
+
+
+def fused_kernel(
+    shards,
+    uly,
+    picks_ref,
+    q_ref,
+    k_ref,
+    v_ref,
+    o_ref,
+    g_ref,
+    dq_ref,
+    dk_ref,
+    dv_ref,
+    held,
+    delta_send,
+    delta_recv,
+    bias,
+    stats,
+    scores,
+    probs_low,
+    score_grads,
+    acc,
+    outgoing,
+    zs,
+    zr,
+    zl,
+    ds_sem,
+    dr_sem,
+    fs,
+    fr,
+    ss,
+    sr,
+    os_sem,
+    or_sem,
+    ol,
+):
+    tok = q_ref.shape[0]
+    length = tok * uly
+    per = length // BLOCK
+    gp = BLOCK // tok
+    blocks = per * shards
+    scale = HD ** (-0.5)
+    b = lax.axis_index("blk")
+    u = lax.axis_index("uly")
+    inputs = {KEY: k_ref, QUERY: q_ref, VALUE: v_ref, GRAD: g_ref}
+    f32 = jnp.float32
+
+    def peer(step):
+        return lax.rem(u + step, uly)
+
+    def cols(p):
+        return pl.ds(pl.multiple_of(p * HD, HD), HD)
+
+    def rows(p):
+        return pl.ds(pl.multiple_of(p * tok, tok), tok)
+
+    def block_rows(c):
+        return pl.ds(pl.multiple_of(c * BLOCK, BLOCK), BLOCK)
+
+    def z_copy(t, p, sender):
+        return pltpu.make_async_remote_copy(
+            src_ref=inputs[t].at[:, cols(p)],
+            dst_ref=held.at[t, b, rows(sender), :],
+            send_sem=zs.at[t, p],
+            recv_sem=zr.at[t, sender],
+            device_id={"blk": b, "uly": p},
+            device_id_type=pl.DeviceIdType.MESH,
+        )
+
+    def d_copy(p, sender):
+        return pltpu.make_async_remote_copy(
+            src_ref=delta_send.at[p],
+            dst_ref=delta_recv.at[sender],
+            send_sem=ds_sem.at[p],
+            recv_sem=dr_sem.at[sender],
+            device_id={"blk": b, "uly": p},
+            device_id_type=pl.DeviceIdType.MESH,
+        )
+
+    def f_copy(t, c, to, sender):
+        return pltpu.make_async_remote_copy(
+            src_ref=held.at[t, sender, block_rows(c), :],
+            dst_ref=held.at[t, sender, block_rows(c), :],
+            send_sem=fs.at[t, c, to],
+            recv_sem=fr.at[t, c, sender],
+            device_id={"blk": to, "uly": u},
+            device_id_type=pl.DeviceIdType.MESH,
+        )
+
+    def s_copy(to, sender):
+        return pltpu.make_async_remote_copy(
+            src_ref=stats.at[sender],
+            dst_ref=stats.at[sender],
+            send_sem=ss.at[to],
+            recv_sem=sr.at[sender],
+            device_id={"blk": to, "uly": u},
+            device_id_type=pl.DeviceIdType.MESH,
+        )
+
+    results = (dq_ref, dk_ref, dv_ref)
+
+    def o_copy(t, p, sender):
+        return pltpu.make_async_remote_copy(
+            src_ref=outgoing.at[t, rows(p), :],
+            dst_ref=results[t].at[:, cols(sender)],
+            send_sem=os_sem.at[t, p],
+            recv_sem=or_sem.at[t, sender],
+            device_id={"blk": b, "uly": p},
+            device_id_type=pl.DeviceIdType.MESH,
+        )
+
+    def o_local(t):
+        return pltpu.make_async_copy(
+            outgoing.at[t, rows(u), :], results[t].at[:, cols(u)], ol.at[t]
+        )
+
+    def z_local(t):
+        return pltpu.make_async_copy(inputs[t].at[:, cols(u)], held.at[t, b, rows(u), :], zl.at[t])
+
+    barrier = pltpu.get_barrier_semaphore()
+    for step in range(1, uly):
+        pl.semaphore_signal(
+            barrier,
+            inc=1,
+            device_id={"blk": b, "uly": peer(step)},
+            device_id_type=pl.DeviceIdType.MESH,
+        )
+    for step in range(1, shards):
+        pl.semaphore_signal(
+            barrier,
+            inc=1,
+            device_id={"blk": lax.rem(b + step, shards), "uly": u},
+            device_id_type=pl.DeviceIdType.MESH,
+        )
+    pl.semaphore_wait(barrier, uly - 1 + shards - 1)
+
+    middle = uly // 2
+    far_first = sorted(range(1, uly), key=lambda step: abs(step - middle))
+    for t in (KEY, QUERY, VALUE, GRAD):
+        for step in far_first:
+            z_copy(t, peer(step), u).start()
+        z_local(t).start()
+
+    product = o_ref[...].astype(f32) * g_ref[...].astype(f32)
+    high = product.astype(jnp.bfloat16)
+    low = (product - high.astype(f32)).astype(jnp.bfloat16)
+    head_of = lax.broadcasted_iota(jnp.int32, (uly, uly * HD), 1) // HD
+    pick_head = jnp.where(
+        head_of == lax.broadcasted_iota(jnp.int32, (uly, uly * HD), 0), 1.0, 0.0
+    ).astype(jnp.bfloat16)
+    sums = lax.dot_general(
+        pick_head, jnp.concatenate([high] * gp, axis=0), ROWS_BY_COLS, preferred_element_type=f32
+    ) + lax.dot_general(
+        pick_head, jnp.concatenate([low] * gp, axis=0), ROWS_BY_COLS, preferred_element_type=f32
+    )
+    place = lax.broadcasted_iota(jnp.int32, (uly, BLOCK), 1) // tok
+    sums = jnp.where(place == lax.rem(u, gp), sums, 0.0)
+    for head in range(uly):
+        delta_send[head] = sums[head : head + 1]
+    for step in far_first:
+        d_copy(peer(step), u).start()
+    delta_recv[u] = delta_send[u]
+
+    lane_block = lax.broadcasted_iota(jnp.int32, (1, length), 1) // BLOCK
+    key_block = lax.broadcasted_iota(jnp.int32, (blocks, length), 0)
+    for s in range(shards):
+        query_block = lane_block + s * per
+        hit = (key_block == query_block) | (key_block == query_block - 1) | (key_block == 0)
+        for r in range(RAND):
+            named = jnp.zeros((1, length), jnp.int32)
+            for i in range(per):
+                named = jnp.where(lane_block == i, picks_ref[s * per + i, r], named)
+            hit = hit | (key_block == named)
+        hit = hit & (key_block <= query_block)
+        bias[s] = jnp.where(hit, 0.0, NEG)
+
+    own_block = u // gp
+
+    def forward(t):
+        z_local(t).wait()
+        for offset in swing(per):
+            c = lax.rem(own_block + offset, per)
+            for i in range(gp):
+                p = c * gp + i
+
+                @pl.when(p != u)
+                def _():
+                    z_copy(t, p, p).wait_recv()
+
+            for to in range(shards):
+                goes = (to > b) if t in (KEY, VALUE) else (to < b)
+
+                @pl.when(goes)
+                def _():
+                    f_copy(t, c, to, b).start()
+
+    def tile_scores(s_key, s_query, jb):
+        keys = held[KEY, s_key, pl.ds(jb * BLOCK, BLOCK), :]
+        tile = lax.dot_general(
+            keys, held[QUERY, s_query], ROWS_BY_COLS, preferred_element_type=f32
+        )
+        return tile * scale + bias[s_query, pl.ds(s_key * per + jb, 1), :]
+
+    forward(KEY)
+    forward(QUERY)
+
+    top = jnp.full((1, length), NEG, f32)
+    for jb in range(per):
+        tile = tile_scores(b, b, jb)
+        key_at = lax.broadcasted_iota(jnp.int32, (BLOCK, length), 0) + jb * BLOCK
+        query_at = lax.broadcasted_iota(jnp.int32, (BLOCK, length), 1)
+        tile = jnp.where(key_at <= query_at, tile, NEG)
+        scores[b, pl.ds(jb * BLOCK, BLOCK), :] = tile
+        top = jnp.maximum(top, jnp.max(tile, axis=0, keepdims=True))
+
+    forward(VALUE)
+    forward(GRAD)
+
+    def far_scores(s, top):
+        for jb in range(per):
+            f_copy(KEY, jb, b, s).wait_recv()
+            tile = tile_scores(s, b, jb)
+            scores[s, pl.ds(jb * BLOCK, BLOCK), :] = tile
+            top = jnp.maximum(top, jnp.max(tile, axis=0, keepdims=True))
+        return top
+
+    top = lax.fori_loop(0, b, far_scores, top)
+
+    def add_exp(s, total):
+        for jb in range(per):
+            tile = jnp.exp(scores[s, pl.ds(jb * BLOCK, BLOCK), :] - top)
+            total = total + jnp.sum(tile, axis=0, keepdims=True)
+        return total
+
+    total = lax.fori_loop(0, b + 1, add_exp, jnp.zeros((1, length), f32))
+    log_total = top + jnp.log(total)
+    for step in range(1, uly):
+        d_copy(peer(step), peer(step)).wait_recv()
+    pieces = []
+    for c in range(per):
+        piece = delta_recv[c * gp]
+        for i in range(1, gp):
+            piece = piece + delta_recv[c * gp + i]
+        pieces.append(piece)
+    delta = jnp.concatenate(pieces, axis=1)
+    stats[b, 0:1, :] = log_total
+    stats[b, 1:2, :] = delta
+    for to in range(shards):
+
+        @pl.when(to < b)
+        def _():
+            s_copy(to, b).start()
+
+    def tile_grads(tile, s_key, s_query, jb, log_row, delta_row):
+        probs = jnp.exp(tile - log_row)
+        values = held[VALUE, s_key, pl.ds(jb * BLOCK, BLOCK), :]
+        prob_grad = lax.dot_general(
+            values, held[GRAD, s_query], ROWS_BY_COLS, preferred_element_type=f32
+        )
+        grads = (probs * (prob_grad - delta_row) * scale).astype(jnp.bfloat16)
+        return probs.astype(jnp.bfloat16), grads
+
+    for jb in range(per):
+        probs, grads = tile_grads(
+            scores[b, pl.ds(jb * BLOCK, BLOCK), :], b, b, jb, log_total, delta
+        )
+        probs_low[pl.ds(jb * BLOCK, BLOCK), :] = probs
+        score_grads[pl.ds(jb * BLOCK, BLOCK), :] = grads
+    acc[0] = lax.dot_general(
+        score_grads[...], held[KEY, b], COLS_BY_COLS, preferred_element_type=f32
+    )
+    acc[1] = jnp.dot(score_grads[...], held[QUERY, b], preferred_element_type=f32)
+    acc[2] = jnp.dot(probs_low[...], held[GRAD, b], preferred_element_type=f32)
+
+    def far_keys(s, carry):
+        for jb in range(per):
+            f_copy(VALUE, jb, b, s).wait_recv()
+            _, grads = tile_grads(
+                scores[s, pl.ds(jb * BLOCK, BLOCK), :], s, b, jb, log_total, delta
+            )
+            score_grads[pl.ds(jb * BLOCK, BLOCK), :] = grads
+        acc[0] += lax.dot_general(
+            score_grads[...], held[KEY, s], COLS_BY_COLS, preferred_element_type=f32
+        )
+        return carry
+
+    lax.fori_loop(0, b, far_keys, 0)
+
+    def send_result(t):
+        outgoing[t] = acc[t].astype(jnp.bfloat16)
+        for step in far_first:
+            o_copy(t, peer(step), u).start()
+        o_local(t).start()
+
+    send_result(0)
+
+    def far_queries(s, carry):
+        for c in range(per):
+            f_copy(QUERY, c, b, s).wait_recv()
+            f_copy(GRAD, c, b, s).wait_recv()
+        s_copy(b, s).wait_recv()
+        log_row = stats[s, 0:1, :]
+        delta_row = stats[s, 1:2, :]
+        for jb in range(per):
+            probs, grads = tile_grads(tile_scores(b, s, jb), b, s, jb, log_row, delta_row)
+            probs_low[pl.ds(jb * BLOCK, BLOCK), :] = probs
+            score_grads[pl.ds(jb * BLOCK, BLOCK), :] = grads
+        acc[1] += jnp.dot(score_grads[...], held[QUERY, s], preferred_element_type=f32)
+        acc[2] += jnp.dot(probs_low[...], held[GRAD, s], preferred_element_type=f32)
+        return carry
+
+    lax.fori_loop(b + 1, shards, far_queries, 0)
+    send_result(1)
+    send_result(2)
+
+    for step in range(1, uly):
+        p = peer(step)
+        d_copy(p, u).wait_send()
+        for t in (KEY, QUERY, VALUE, GRAD):
+            z_copy(t, p, u).wait_send()
+    for to in range(shards):
+
+        @pl.when(to > b)
+        def _():
+            for c in range(per):
+                f_copy(KEY, c, to, b).wait_send()
+                f_copy(VALUE, c, to, b).wait_send()
+
+        @pl.when(to < b)
+        def _():
+            for c in range(per):
+                f_copy(QUERY, c, to, b).wait_send()
+                f_copy(GRAD, c, to, b).wait_send()
+            s_copy(to, b).wait_send()
+
+    for t in range(3):
+        o_local(t).wait()
+        for step in range(1, uly):
+            p = peer(step)
+            o_copy(t, p, p).wait_recv()
+            o_copy(t, p, u).wait_send()
+
+
+def fused_on_device(shards, uly, q, k, v, o, g, random_blocks):
+    tok, width = q.shape
+    length = tok * uly
+    per = length // BLOCK
+    dma = pltpu.SemaphoreType.DMA
+    vmem = pl.BlockSpec(memory_space=pltpu.VMEM)
+    return pl.pallas_call(
+        functools.partial(fused_kernel, shards, uly),
+        out_shape=[jax.ShapeDtypeStruct((tok, width), jnp.bfloat16)] * 3,
+        in_specs=[pl.BlockSpec(memory_space=pltpu.SMEM)] + [vmem] * 5,
+        out_specs=[vmem] * 3,
+        scratch_shapes=[
+            pltpu.VMEM((4, shards, length, HD), jnp.bfloat16),
+            pltpu.VMEM((uly, 1, BLOCK), jnp.float32),
+            pltpu.VMEM((uly, 1, BLOCK), jnp.float32),
+            pltpu.VMEM((shards, shards * per, length), jnp.float32),
+            pltpu.VMEM((shards, 2, length), jnp.float32),
+            pltpu.VMEM((shards, length, length), jnp.float32),
+            pltpu.VMEM((length, length), jnp.bfloat16),
+            pltpu.VMEM((length, length), jnp.bfloat16),
+            pltpu.VMEM((3, length, HD), jnp.float32),
+            pltpu.VMEM((3, length, HD), jnp.bfloat16),
+            dma((4, uly)),
+            dma((4, uly)),
+            dma((4,)),
+            dma((uly,)),
+            dma((uly,)),
+            dma((4, per, shards)),
+            dma((4, per, shards)),
+            dma((shards,)),
+            dma((shards,)),
+            dma((3, uly)),
+            dma((3, uly)),
+            dma((3,)),
+        ],
+        compiler_params=pltpu.CompilerParams(
+            collective_id=0, has_side_effects=True, vmem_limit_bytes=40 * 1024 * 1024
+        ),
+    )(random_blocks, q, k, v, o, g)
+
+
+def wide_or_fused(shards, uly, *operands):
+    tok, width = operands[0].shape
+    length = tok * uly
+    fits = shards * length * length * 4 <= 16 * 1024 * 1024
+    if fits and width == uly * HD and BLOCK % tok == 0 and length % BLOCK == 0:
+        return tuple(fused_on_device(shards, uly, *operands))
+    return on_device(*operands)
+
+
 def solution(mesh):
     return jax.shard_map(
-        on_device,
+        functools.partial(wide_or_fused, mesh.shape["blk"], mesh.shape["uly"]),
         mesh=mesh,
         in_specs=(
             P(("blk", "uly"), None),

time: 173 us -> 45.2 us (0.26)
  waiting for transfers between devices: 59.7 us -> 0 us
  starting transfers between devices: 48.3 us -> 0 us
  Pallas kernels: 0 us -> 36.8 us
  other arithmetic: 31.3 us -> 0 us
  local copies, waits for them, and re-layouts: 21.6 us -> 7.24 us
  matrix products: 8.85 us -> 0 us
    all_to_all x12 -> x0, waiting for transfers between devices: 59.7 us -> none  [the longest x1 11.4 us: on_device(): lax.all_to_all(jnp.concatenate([far_key_grad, extra_key_grad], axis=1), '...]
    all_to_all x12 -> x0, starting transfers between devices: 48.3 us -> none  [the longest x1 6.35 us: on_device(): lax.all_to_all(to_heads(key_proj), 'uly', split_axis=1, concat_axis=0, ti...]
    pallas_call x0 -> x1, Pallas kernels: none -> 36.8 us  [fused_on_device(): pl.pallas_call(functools.partial(fused_kernel, shards, uly), out_shape=[j...]
    scatter-add x8 -> x0, other arithmetic: 10.2 us -> none  [the longest x1 4.48 us: group_turn(): key_grad_store.at[index_grp]]
    dot_general x5 -> x0, matrix products: 8.85 us -> none  [the longest x1 2.44 us: group_turn(): jnp.einsum('gqk,gkd->gqd', score_grad, key_sel, preferred_element_type=jn...]
    select_n x13 -> x0, other arithmetic: 8.09 us -> none  [the longest x1 2.02 us: on_device(): jnp.where(filled[:, :, None, None], back_value, 0.0)]
    reshape x9 -> x0, local copies, waits for them, and re-layouts: 5.52 us -> none  [the longest x5 5.19 us: to_heads(): return tensor.reshape(tok_count, head_count, HD)]
    concatenate x8 -> x0, other arithmetic: 4.1 us -> none  [the longest x1 1.11 us: on_device(): jnp.concatenate([far_value_grad, extra_value_grad], axis=1)]
  transfers between devices with their start and end apart: 12 -> 0, of which waited for: 11 -> 0; matrix products, arithmetic and copies ran while one was open for 22% -> 0% of each run, Pallas kernels for 0% -> 0%
where the time goes in v1:
time: 45.2 us; the launch traced here: 44.7 us
  Pallas kernels  36.8 us (81%)
  local copies, waits for them, and re-layouts  7.24 us (16%)
  between operations  0.64 us (1%)
    pallas_call x1, Pallas kernels, fused_on_device(): pl.pallas_call(functools.partial(fused_kernel, shards, uly), out_shape=[j...  36.8 us
    unnamed x14, local copies, waits for them, and re-layouts  7.24 us

profile of v1, /device:TPU:0, one launch (start us, length us, event | category | flops | bytes accessed | tf_op | source)
XLA Modules:
  0.0 44.7 jit_solution(18144624679029462224)
XLA Ops:
  0.6 0.8 %copy.9.picks_ref = s32[16,3]{1,0:T(8,128)S(1)} copy(s32[16,3]{0,1:T(4,128)} %param.11) | data formatting | bytes 384 | tf_op args[5]
  1.4 0.0 copy-start
  1.4 0.9 %copy-done = bf16[64,1024]{1,0:T(8,128)(2,1)S(1)} copy-done((bf16[64,1024]{1,0:T(8,128)(2,1)S(1)}, bf16[64,1024]{1,0:T(8,128)(2,1)}, u32[]{:S(2)}) %copy-start) | copy-done | bytes 131096
  2.3 0.0 copy-start.1
  2.3 0.9 %copy-done.1 = bf16[64,1024]{1,0:T(8,128)(2,1)S(1)} copy-done((bf16[64,1024]{1,0:T(8,128)(2,1)S(1)}, bf16[64,1024]{1,0:T(8,128)(2,1)}, u32[]{:S(2)}) %copy-start.1) | copy-done | bytes 131096
  3.2 0.0 copy-start.2
  3.2 0.9 %copy-done.2 = bf16[64,1024]{1,0:T(8,128)(2,1)S(1)} copy-done((bf16[64,1024]{1,0:T(8,128)(2,1)S(1)}, bf16[64,1024]{1,0:T(8,128)(2,1)}, u32[]{:S(2)}) %copy-start.2) | copy-done | bytes 131096
  4.1 0.0 copy-start.3
  4.1 0.9 %copy-done.3 = bf16[64,1024]{1,0:T(8,128)(2,1)S(1)} copy-done((bf16[64,1024]{1,0:T(8,128)(2,1)S(1)}, bf16[64,1024]{1,0:T(8,128)(2,1)}, u32[]{:S(2)}) %copy-start.3) | copy-done | bytes 131096
  5.0 0.0 copy-start.4
  5.0 0.9 %copy-done.4 = bf16[64,1024]{1,0:T(8,128)(2,1)S(1)} copy-done((bf16[64,1024]{1,0:T(8,128)(2,1)S(1)}, bf16[64,1024]{1,0:T(8,128)(2,1)}, u32[]{:S(2)}) %copy-start.4) | copy-done | bytes 131096
  5.9 36.8 %shard_map.85 = (bf16[64,1024]{1,0:T(8,128)(2,1)S(1)}, bf16[64,1024]{1,0:T(8,128)(2,1)S(1)}, bf16[64,1024]{1,0:T(8,128)(2,1)S(1)}) custom-call(s32[16,3]{1,0:T(8,128)S(1)} %copy.9.picks_ref, bf16[64,1024]{1,0:T(8,128)(2,1)S(1)} %copy-done, bf16[64,1024]{1,0:T(8,128)(2,1)S(1)} %copy-done.1, bf16[64,1024]{1,0:T(8,128)(2,1)S(1)} %copy-done.2, ...), custom_call_target="tpu_custom_call" | custom-call | tf_op jit(solution)/shard_map/pallas_call | solution.py:655
  42.7 0.7 %copy.13 = bf16[64,1024]{1,0:T(8,128)(2,1)} copy(bf16[64,1024]{1,0:T(8,128)(2,1)S(1)} %get-tuple-element.6) | data formatting | bytes 262144
  43.4 0.7 %copy.14 = bf16[64,1024]{1,0:T(8,128)(2,1)} copy(bf16[64,1024]{1,0:T(8,128)(2,1)S(1)} %get-tuple-element.7) | data formatting | bytes 262144
  44.0 0.7 %copy.15 = bf16[64,1024]{1,0:T(8,128)(2,1)} copy(bf16[64,1024]{1,0:T(8,128)(2,1)S(1)} %get-tuple-element.8) | data formatting | bytes 262144
Async XLA Ops:
  1.4 0.9 %copy-start = (bf16[64,1024]{1,0:T(8,128)(2,1)S(1)}, bf16[64,1024]{1,0:T(8,128)(2,1)}, u32[]{:S(2)}) copy-start(bf16[64,1024]{1,0:T(8,128)(2,1)} %q_ref.1) | copy-start | bytes 393220
  2.3 0.9 %copy-start.1 = (bf16[64,1024]{1,0:T(8,128)(2,1)S(1)}, bf16[64,1024]{1,0:T(8,128)(2,1)}, u32[]{:S(2)}) copy-start(bf16[64,1024]{1,0:T(8,128)(2,1)} %k_ref.1) | copy-start | bytes 393220
  3.2 0.9 %copy-start.2 = (bf16[64,1024]{1,0:T(8,128)(2,1)S(1)}, bf16[64,1024]{1,0:T(8,128)(2,1)}, u32[]{:S(2)}) copy-start(bf16[64,1024]{1,0:T(8,128)(2,1)} %v_ref.1) | copy-start | bytes 393220
  4.1 0.9 %copy-start.3 = (bf16[64,1024]{1,0:T(8,128)(2,1)S(1)}, bf16[64,1024]{1,0:T(8,128)(2,1)}, u32[]{:S(2)}) copy-start(bf16[64,1024]{1,0:T(8,128)(2,1)} %o_ref.1) | copy-start | bytes 393220
  5.0 0.9 %copy-start.4 = (bf16[64,1024]{1,0:T(8,128)(2,1)S(1)}, bf16[64,1024]{1,0:T(8,128)(2,1)}, u32[]{:S(2)}) copy-start(bf16[64,1024]{1,0:T(8,128)(2,1)} %g_ref.1) | copy-start | bytes 393220

commit v2 on v1

--- a/solution.py
+++ b/solution.py
@@ -316,6 +316,7 @@
     dq_ref,
     dk_ref,
     dv_ref,
+    rows_in,
     held,
     delta_send,
     delta_recv,
@@ -338,6 +339,7 @@
     os_sem,
     or_sem,
     ol,
+    il,
 ):
     tok = q_ref.shape[0]
     length = tok * uly
@@ -422,6 +424,12 @@
     def z_local(t):
         return pltpu.make_async_copy(inputs[t].at[:, cols(u)], held.at[t, b, rows(u), :], zl.at[t])
 
+    fetches = (
+        pltpu.make_async_copy(o_ref, rows_in.at[0], il.at[0]),
+        pltpu.make_async_copy(g_ref, rows_in.at[1], il.at[1]),
+    )
+    for fetch in fetches:
+        fetch.start()
     barrier = pltpu.get_barrier_semaphore()
     for step in range(1, uly):
         pl.semaphore_signal(
@@ -446,7 +454,9 @@
             z_copy(t, peer(step), u).start()
         z_local(t).start()
 
-    product = o_ref[...].astype(f32) * g_ref[...].astype(f32)
+    for fetch in fetches:
+        fetch.wait()
+    product = rows_in[0].astype(f32) * rows_in[1].astype(f32)
     high = product.astype(jnp.bfloat16)
     low = (product - high.astype(f32)).astype(jnp.bfloat16)
     head_of = lax.broadcasted_iota(jnp.int32, (uly, uly * HD), 1) // HD
@@ -474,7 +484,7 @@
         for r in range(RAND):
             named = jnp.zeros((1, length), jnp.int32)
             for i in range(per):
-                named = jnp.where(lane_block == i, picks_ref[s * per + i, r], named)
+                named = jnp.where(lane_block == i, picks_ref[r, s * per + i], named)
             hit = hit | (key_block == named)
         hit = hit & (key_block <= query_block)
         bias[s] = jnp.where(hit, 0.0, NEG)
@@ -646,18 +656,25 @@
             o_copy(t, p, u).wait_send()
 
 
+def write_out(a_ref, b_ref, c_ref, a_out, b_out, c_out):
+    a_out[...] = a_ref[...]
+    b_out[...] = b_ref[...]
+    c_out[...] = c_ref[...]
+
+
 def fused_on_device(shards, uly, q, k, v, o, g, random_blocks):
     tok, width = q.shape
     length = tok * uly
     per = length // BLOCK
     dma = pltpu.SemaphoreType.DMA
-    vmem = pl.BlockSpec(memory_space=pltpu.VMEM)
-    return pl.pallas_call(
+    hbm = pl.BlockSpec(memory_space=pltpu.HBM)
+    results = pl.pallas_call(
         functools.partial(fused_kernel, shards, uly),
         out_shape=[jax.ShapeDtypeStruct((tok, width), jnp.bfloat16)] * 3,
-        in_specs=[pl.BlockSpec(memory_space=pltpu.SMEM)] + [vmem] * 5,
-        out_specs=[vmem] * 3,
+        in_specs=[pl.BlockSpec(memory_space=pltpu.SMEM)] + [hbm] * 5,
+        out_specs=[hbm] * 3,
         scratch_shapes=[
+            pltpu.VMEM((2, tok, width), jnp.bfloat16),
             pltpu.VMEM((4, shards, length, HD), jnp.bfloat16),
             pltpu.VMEM((uly, 1, BLOCK), jnp.float32),
             pltpu.VMEM((uly, 1, BLOCK), jnp.float32),
@@ -680,11 +697,20 @@
             dma((3, uly)),
             dma((3, uly)),
             dma((3,)),
+            dma((2,)),
         ],
         compiler_params=pltpu.CompilerParams(
-            collective_id=0, has_side_effects=True, vmem_limit_bytes=40 * 1024 * 1024
+            collective_id=0, has_side_effects=True, vmem_limit_bytes=67043328
         ),
-    )(random_blocks, q, k, v, o, g)
+    )(random_blocks.T, q, k, v, o, g)
+    vmem = pl.BlockSpec(memory_space=pltpu.VMEM)
+    return pl.pallas_call(
+        write_out,
+        out_shape=[jax.ShapeDtypeStruct((tok, width), jnp.bfloat16)] * 3,
+        in_specs=[vmem] * 3,
+        out_specs=[vmem] * 3,
+        compiler_params=pltpu.CompilerParams(vmem_limit_bytes=67043328),
+    )(*results)
 
 
 def wide_or_fused(shards, uly, *operands):

time: 45.2 us -> 40.1 us (0.89)
  local copies, waits for them, and re-layouts: 7.24 us -> 0 us
  Pallas kernels: 36.8 us -> 39 us
    unnamed x14 -> x0, local copies, waits for them, and re-layouts: 7.24 us -> none
    pallas_call x0 -> x1, Pallas kernels: none -> 1.78 us  [fused_on_device(): pl.pallas_call(write_out, out_shape=[jax.ShapeDtypeStruct((tok, width), j...]
where the time goes in v2:
time: 40.1 us; the launch traced here: 39.6 us
  Pallas kernels  39 us (97%)
  between operations  0.64 us (2%)
    pallas_call x1, Pallas kernels, fused_on_device(): pl.pallas_call(functools.partial(fused_kernel, shards, uly), out_shape=[j...  37.2 us
    pallas_call x1, Pallas kernels, fused_on_device(): pl.pallas_call(write_out, out_shape=[jax.ShapeDtypeStruct((tok, width), j...  1.78 us

profile of v2, /device:TPU:0, one launch (start us, length us, event | category | flops | bytes accessed | tf_op | source)
XLA Modules:
  0.0 39.6 jit_solution(10512124828035353754)
XLA Ops:
  0.6 37.2 %shard_map.85 = (bf16[64,1024]{1,0:T(8,128)(2,1)}, bf16[64,1024]{1,0:T(8,128)(2,1)}, bf16[64,1024]{1,0:T(8,128)(2,1)}) custom-call(s32[3,16]{1,0:T(4,128)} %bitcast.1, bf16[64,1024]{1,0:T(8,128)(2,1)} %q_ref.1, bf16[64,1024]{1,0:T(8,128)(2,1)} %k_ref.1, bf16[64,1024]{1,0:T(8,128)(2,1)} %v_ref.1, bf16[64,1024]{1,0:T(8,128)(2,1)} %o_ref.1, bf16[64,1024]{1,0:T(8,128)(2,1)} %g_ref.1), custom_call_target="tpu_custom_call" | custom-call | tf_op jit(solution)/shard_map/pallas_call | solution.py:671
  37.8 1.8 %shard_map.86 = (bf16[64,1024]{1,0:T(8,128)(2,1)}, bf16[64,1024]{1,0:T(8,128)(2,1)}, bf16[64,1024]{1,0:T(8,128)(2,1)}) custom-call(bf16[64,1024]{1,0:T(8,128)(2,1)} %get-tuple-element.6.a_ref, bf16[64,1024]{1,0:T(8,128)(2,1)} %get-tuple-element.7.b_ref, bf16[64,1024]{1,0:T(8,128)(2,1)} %get-tuple-element.8.c_ref), custom_call_target="tpu_custom_call" | custom-call | tf_op jit(solution)/shard_map/pallas_call | solution.py:707

commit v3 on v2

--- a/solution.py
+++ b/solution.py
@@ -297,17 +297,10 @@
 COLS_BY_COLS = (((0,), (0,)), ((), ()))
 
 
-def swing(count):
-    offsets = [0]
-    for step in range(1, count):
-        offsets.append((step + 1) // 2 if step % 2 else count - step // 2)
-    return offsets
-
-
 def fused_kernel(
     shards,
     uly,
-    picks_ref,
+    picks_hbm,
     q_ref,
     k_ref,
     v_ref,
@@ -316,6 +309,7 @@
     dq_ref,
     dk_ref,
     dv_ref,
+    picks_ref,
     rows_in,
     held,
     delta_send,
@@ -355,6 +349,19 @@
     def peer(step):
         return lax.rem(u + step, uly)
 
+    def swap_order(count, at=None):
+        at = u if at is None else at
+        if count & (count - 1):
+            return [lax.rem(at + step, count) for step in range(1, count)]
+        order = []
+        for mask in range(1, count):
+            other = at
+            for bit in range(count.bit_length() - 1):
+                if mask >> bit & 1:
+                    other = other + (1 << bit) * (1 - 2 * (at // (1 << bit) % 2))
+            order.append(other)
+        return order
+
     def cols(p):
         return pl.ds(pl.multiple_of(p * HD, HD), HD)
 
@@ -427,6 +434,7 @@
     fetches = (
         pltpu.make_async_copy(o_ref, rows_in.at[0], il.at[0]),
         pltpu.make_async_copy(g_ref, rows_in.at[1], il.at[1]),
+        pltpu.make_async_copy(picks_hbm, picks_ref, il.at[2]),
     )
     for fetch in fetches:
         fetch.start()
@@ -445,15 +453,6 @@
             device_id={"blk": lax.rem(b + step, shards), "uly": u},
             device_id_type=pl.DeviceIdType.MESH,
         )
-    pl.semaphore_wait(barrier, uly - 1 + shards - 1)
-
-    middle = uly // 2
-    far_first = sorted(range(1, uly), key=lambda step: abs(step - middle))
-    for t in (KEY, QUERY, VALUE, GRAD):
-        for step in far_first:
-            z_copy(t, peer(step), u).start()
-        z_local(t).start()
-
     for fetch in fetches:
         fetch.wait()
     product = rows_in[0].astype(f32) * rows_in[1].astype(f32)
@@ -472,8 +471,6 @@
     sums = jnp.where(place == lax.rem(u, gp), sums, 0.0)
     for head in range(uly):
         delta_send[head] = sums[head : head + 1]
-    for step in far_first:
-        d_copy(peer(step), u).start()
     delta_recv[u] = delta_send[u]
 
     lane_block = lax.broadcasted_iota(jnp.int32, (1, length), 1) // BLOCK
@@ -489,25 +486,37 @@
         hit = hit & (key_block <= query_block)
         bias[s] = jnp.where(hit, 0.0, NEG)
 
+    pl.semaphore_wait(barrier, uly - 1 + shards - 1)
+    z_order = swap_order(uly)
+    for pair in ((KEY, QUERY), (VALUE, GRAD)):
+        for t in pair:
+            z_local(t).start()
+        for p in z_order:
+            for t in pair:
+                z_copy(t, p, u).start()
+    for p in z_order:
+        d_copy(p, u).start()
+
     own_block = u // gp
 
-    def forward(t):
-        z_local(t).wait()
-        for offset in swing(per):
-            c = lax.rem(own_block + offset, per)
-            for i in range(gp):
-                p = c * gp + i
-
-                @pl.when(p != u)
-                def _():
-                    z_copy(t, p, p).wait_recv()
-
-            for to in range(shards):
-                goes = (to > b) if t in (KEY, VALUE) else (to < b)
-
-                @pl.when(goes)
-                def _():
-                    f_copy(t, c, to, b).start()
+    def forward(pair):
+        for t in pair:
+            z_local(t).wait()
+        for c in [own_block] + swap_order(per, own_block):
+            for t in pair:
+                for i in range(gp):
+                    p = c * gp + i
+
+                    @pl.when(p != u)
+                    def _():
+                        z_copy(t, p, p).wait_recv()
+
+                for to in range(shards):
+                    goes = (to > b) if t in (KEY, VALUE) else (to < b)
+
+                    @pl.when(goes)
+                    def _():
+                        f_copy(t, c, to, b).start()
 
     def tile_scores(s_key, s_query, jb):
         keys = held[KEY, s_key, pl.ds(jb * BLOCK, BLOCK), :]
@@ -516,8 +525,7 @@
         )
         return tile * scale + bias[s_query, pl.ds(s_key * per + jb, 1), :]
 
-    forward(KEY)
-    forward(QUERY)
+    forward((KEY, QUERY))
 
     top = jnp.full((1, length), NEG, f32)
     for jb in range(per):
@@ -528,8 +536,7 @@
         scores[b, pl.ds(jb * BLOCK, BLOCK), :] = tile
         top = jnp.maximum(top, jnp.max(tile, axis=0, keepdims=True))
 
-    forward(VALUE)
-    forward(GRAD)
+    forward((VALUE, GRAD))
 
     def far_scores(s, top):
         for jb in range(per):
@@ -587,6 +594,17 @@
     acc[1] = jnp.dot(score_grads[...], held[QUERY, b], preferred_element_type=f32)
     acc[2] = jnp.dot(probs_low[...], held[GRAD, b], preferred_element_type=f32)
 
+    def send_result(t):
+        outgoing[t] = acc[t].astype(jnp.bfloat16)
+        for p in z_order:
+            o_copy(t, p, u).start()
+        o_local(t).start()
+
+    @pl.when(b == shards - 1)
+    def _():
+        send_result(1)
+        send_result(2)
+
     def far_keys(s, carry):
         for jb in range(per):
             f_copy(VALUE, jb, b, s).wait_recv()
@@ -600,12 +618,6 @@
         return carry
 
     lax.fori_loop(0, b, far_keys, 0)
-
-    def send_result(t):
-        outgoing[t] = acc[t].astype(jnp.bfloat16)
-        for step in far_first:
-            o_copy(t, peer(step), u).start()
-        o_local(t).start()
 
     send_result(0)
 
@@ -624,9 +636,12 @@
         acc[2] += jnp.dot(probs_low[...], held[GRAD, s], preferred_element_type=f32)
         return carry
 
-    lax.fori_loop(b + 1, shards, far_queries, 0)
-    send_result(1)
-    send_result(2)
+    @pl.when(b < shards - 1)
+    def _():
+        lax.fori_loop(b + 1, shards, far_queries, 0)
+        send_result(1)
+        send_result(2)
+
 
     for step in range(1, uly):
         p = peer(step)
@@ -671,9 +686,10 @@
     results = pl.pallas_call(
         functools.partial(fused_kernel, shards, uly),
         out_shape=[jax.ShapeDtypeStruct((tok, width), jnp.bfloat16)] * 3,
-        in_specs=[pl.BlockSpec(memory_space=pltpu.SMEM)] + [hbm] * 5,
+        in_specs=[hbm] * 6,
         out_specs=[hbm] * 3,
         scratch_shapes=[
+            pltpu.SMEM(random_blocks.shape[::-1], jnp.int32),
             pltpu.VMEM((2, tok, width), jnp.bfloat16),
             pltpu.VMEM((4, shards, length, HD), jnp.bfloat16),
             pltpu.VMEM((uly, 1, BLOCK), jnp.float32),
@@ -697,7 +713,7 @@
             dma((3, uly)),
             dma((3, uly)),
             dma((3,)),
-            dma((2,)),
+            dma((3,)),
         ],
         compiler_params=pltpu.CompilerParams(
             collective_id=0, has_side_effects=True, vmem_limit_bytes=67043328

time: 40.1 us -> 38 us (0.948)
  Pallas kernels: 39 us -> 37.2 us
    pallas_call x1, Pallas kernels: 37.2 us -> 35.4 us  [fused_on_device(): pl.pallas_call(functools.partial(fused_kernel, shards, uly), out_shape=[j...]
where the time goes in v3:
time: 38 us; the launch traced here: 37.8 us
  Pallas kernels  37.2 us (98%)
  between operations  0.64 us (2%)
    pallas_call x1, Pallas kernels, fused_on_device(): pl.pallas_call(functools.partial(fused_kernel, shards, uly), out_shape=[j...  35.4 us
    pallas_call x1, Pallas kernels, fused_on_device(): pl.pallas_call(write_out, out_shape=[jax.ShapeDtypeStruct((tok, width), j...  1.78 us

profile of v3, /device:TPU:0, one launch (start us, length us, event | category | flops | bytes accessed | tf_op | source)
XLA Modules:
  0.0 37.8 jit_solution(9227813135953516906)
XLA Ops:
  0.6 35.4 %shard_map.85 = (bf16[64,1024]{1,0:T(8,128)(2,1)}, bf16[64,1024]{1,0:T(8,128)(2,1)}, bf16[64,1024]{1,0:T(8,128)(2,1)}) custom-call(s32[3,16]{1,0:T(4,128)} %bitcast.1, bf16[64,1024]{1,0:T(8,128)(2,1)} %q_ref.1, bf16[64,1024]{1,0:T(8,128)(2,1)} %k_ref.1, bf16[64,1024]{1,0:T(8,128)(2,1)} %v_ref.1, bf16[64,1024]{1,0:T(8,128)(2,1)} %o_ref.1, bf16[64,1024]{1,0:T(8,128)(2,1)} %g_ref.1), custom_call_target="tpu_custom_call" | custom-call | tf_op jit(solution)/shard_map/pallas_call | solution.py:686
  36.1 1.8 %shard_map.86 = (bf16[64,1024]{1,0:T(8,128)(2,1)}, bf16[64,1024]{1,0:T(8,128)(2,1)}, bf16[64,1024]{1,0:T(8,128)(2,1)}) custom-call(bf16[64,1024]{1,0:T(8,128)(2,1)} %get-tuple-element.6.a_ref, bf16[64,1024]{1,0:T(8,128)(2,1)} %get-tuple-element.7.b_ref, bf16[64,1024]{1,0:T(8,128)(2,1)} %get-tuple-element.8.c_ref), custom_call_target="tpu_custom_call" | custom-call | tf_op jit(solution)/shard_map/pallas_call | solution.py:723

commit v4 on v3

--- a/solution.py
+++ b/solution.py
@@ -671,10 +671,23 @@
             o_copy(t, p, u).wait_send()
 
 
-def write_out(a_ref, b_ref, c_ref, a_out, b_out, c_out):
-    a_out[...] = a_ref[...]
-    b_out[...] = b_ref[...]
-    c_out[...] = c_ref[...]
+def write_out(a_ref, b_ref, c_ref, a_out, b_out, c_out, held, arrived, done):
+    pairs = ((a_ref, a_out), (b_ref, b_out), (c_ref, c_out))
+    reads = [
+        pltpu.make_async_copy(source, held.at[i], arrived.at[i])
+        for i, (source, _) in enumerate(pairs)
+    ]
+    writes = [
+        pltpu.make_async_copy(held.at[i], target, done.at[i])
+        for i, (_, target) in enumerate(pairs)
+    ]
+    for read in reads:
+        read.start()
+    for read, write in zip(reads, writes):
+        read.wait()
+        write.start()
+    for write in writes:
+        write.wait()
 
 
 def fused_on_device(shards, uly, q, k, v, o, g, random_blocks):
@@ -719,12 +732,12 @@
             collective_id=0, has_side_effects=True, vmem_limit_bytes=67043328
         ),
     )(random_blocks.T, q, k, v, o, g)
-    vmem = pl.BlockSpec(memory_space=pltpu.VMEM)
     return pl.pallas_call(
         write_out,
         out_shape=[jax.ShapeDtypeStruct((tok, width), jnp.bfloat16)] * 3,
-        in_specs=[vmem] * 3,
-        out_specs=[vmem] * 3,
+        in_specs=[hbm] * 3,
+        out_specs=[hbm] * 3,
+        scratch_shapes=[pltpu.VMEM((3, tok, width), jnp.bfloat16), dma((3,)), dma((3,))],
         compiler_params=pltpu.CompilerParams(vmem_limit_bytes=67043328),
     )(*results)
 

time: 38 us -> 38 us (level)
  no operation moved by 1% of the time
where the time goes in v4:
time: 38 us; the launch traced here: 37.8 us
  Pallas kernels  37.2 us (98%)
  between operations  0.64 us (2%)
    pallas_call x1, Pallas kernels, fused_on_device(): pl.pallas_call(functools.partial(fused_kernel, shards, uly), out_shape=[j...  35.4 us
    pallas_call x1, Pallas kernels, fused_on_device(): pl.pallas_call(write_out, out_shape=[jax.ShapeDtypeStruct((tok, width), j...  1.74 us

profile of v4, /device:TPU:0, one launch (start us, length us, event | category | flops | bytes accessed | tf_op | source)
XLA Modules:
  0.0 37.8 jit_solution(10215699688215223282)
XLA Ops:
  0.6 35.4 %shard_map.85 = (bf16[64,1024]{1,0:T(8,128)(2,1)}, bf16[64,1024]{1,0:T(8,128)(2,1)}, bf16[64,1024]{1,0:T(8,128)(2,1)}) custom-call(s32[3,16]{1,0:T(4,128)} %bitcast.1, bf16[64,1024]{1,0:T(8,128)(2,1)} %q_ref.1, bf16[64,1024]{1,0:T(8,128)(2,1)} %k_ref.1, bf16[64,1024]{1,0:T(8,128)(2,1)} %v_ref.1, bf16[64,1024]{1,0:T(8,128)(2,1)} %o_ref.1, bf16[64,1024]{1,0:T(8,128)(2,1)} %g_ref.1), custom_call_target="tpu_custom_call" | custom-call | tf_op jit(solution)/shard_map/pallas_call | solution.py:699
  36.1 1.7 %shard_map.86 = (bf16[64,1024]{1,0:T(8,128)(2,1)}, bf16[64,1024]{1,0:T(8,128)(2,1)}, bf16[64,1024]{1,0:T(8,128)(2,1)}) custom-call(bf16[64,1024]{1,0:T(8,128)(2,1)} %get-tuple-element.6.a_ref, bf16[64,1024]{1,0:T(8,128)(2,1)} %get-tuple-element.7.b_ref, bf16[64,1024]{1,0:T(8,128)(2,1)} %get-tuple-element.8.c_ref), custom_call_target="tpu_custom_call" | custom-call | tf_op jit(solution)/shard_map/pallas_call | solution.py:735
